TPU v7x, 256 devices: a whole 4x4x8 slice. The times are simulated.
256 devices in a mesh: track: 64 (over y, z, core), det: 4 (over x).
Axes of the slice: x: 4, y: 4, z: 8, core: 2. Of those that a mesh axis runs over, the one named last changes fastest.
Arguments:
- jac: float32 [32768, 12, 512], P('track', None, 'det'), may hold values from -1.75 to 1.75
- obs: float32 [32768, 512], P('track', 'det'), may hold values from -6 to 6
- match: int32 [32768], P('track'), may hold values from 0 to 32767, as said below
- tile_knot: int32 [32768], P('track'), may hold values from 0 to 127
- tile_frac: float32 [32768], P('track'), may hold values from 0 to 1
Outputs:
- knot_field: float32 [12, 8192], P(None, 'track')
- tie_residual: float32 [32768, 512], P('track', 'det')
Inputs may be any that keep to these rules, and one draw needn't show every extreme that they name: match[match[i]] = i and match[i] != i; the tiles of each index of track cross exactly 8 tiles of every index of track, itself included.
All inputs are finite; a program needn't handle non-finite values.
Results may differ from a plain program's by a relative error of at most 0.0001.
Values sent between devices are 32-bit elements; how exact they have to be, the bound alone decides.
A program may use at most 64 MiB of HBM per device.

v0:
```python
import jax
import jax.numpy as jnp
from jax import lax
from jax.sharding import PartitionSpec as P

KNOT_DEV = 128
ITERS = 4
damping = 1.0


def passed_along(value, axis, steps):
    count = lax.axis_size(axis)
    leading, last = (max(0, -steps), min(count, count - steps))
    return lax.ppermute(value, axis, [(source, source + steps) for source in range(leading, last)])


def local(jac, obs, match, tile_knot, tile_frac):
    highest = lax.Precision.HIGHEST
    tiles_dev = jac.shape[0]
    params = jac.shape[1]
    n_track = lax.axis_size("track")
    n_det = lax.axis_size("det")
    per_peer = tiles_dev // n_track
    send_order = jnp.argsort(match // tiles_dev, stable=True)

    def arrange(values):
        return values[send_order].reshape((n_track, per_peer) + values.shape[1:])

    slots_in = lax.all_to_all(
        arrange(match % tiles_dev), "track", split_axis=0, concat_axis=0, tiled=True
    )
    receive_order = jnp.argsort(slots_in.reshape(-1))

    def settle(arrived):
        joined = arrived.reshape((tiles_dev,) + arrived.shape[2:])
        return joined[receive_order]

    def partner_values(values):
        return settle(
            lax.all_to_all(arrange(values), "track", split_axis=0, concat_axis=0, tiled=True)
        )

    knot_rows = lax.broadcasted_iota(jnp.int32, (KNOT_DEV, tiles_dev), 0)
    weights = jnp.where(knot_rows == tile_knot[None, :], 1.0 - tile_frac[None, :], 0.0)
    weights = weights + jnp.where(knot_rows == tile_knot[None, :] + 1, tile_frac[None, :], 0.0)
    weights_back = weights.T
    edge_weight = jnp.where(tile_knot == KNOT_DEV - 1, tile_frac, 0.0)
    misfit = obs - partner_values(obs)

    def adjoint(residual_rows):
        partial_value = jnp.einsum("ipw,iw->pi", jac, residual_rows, precision=highest)
        partial_value = lax.psum(partial_value, "det")
        spread = jnp.dot(partial_value, weights_back, precision=highest)
        spill_over = jnp.dot(partial_value, edge_weight, precision=highest)
        carried = passed_along(spill_over, "track", 1)
        return spread.at[:, 0].add(carried)

    def slope_total(gradient):
        return lax.psum(jnp.sum(gradient * gradient), "track")

    knot_field = jnp.zeros((params, KNOT_DEV), jnp.float32)
    tie_residual = misfit
    gradient = adjoint(tie_residual)
    direction = gradient
    slope_norm = slope_total(gradient)
    for iteration in range(ITERS):
        following = passed_along(direction[:, 0], "track", -1)
        interp = (
            jnp.dot(direction, weights, precision=highest)
            + following[:, None] * edge_weight[None, :]
        )
        own_pred = jnp.einsum("ipw,pi->iw", jac, interp, precision=highest)
        other_pred = partner_values(own_pred)
        change = own_pred - other_pred
        change_sq, direction_sq = lax.psum(
            (jnp.sum(change * change), jnp.sum(direction * direction)), ("track", "det")
        )
        curvature = 0.5 * change_sq + damping * direction_sq / n_det
        step_length = slope_norm / curvature
        knot_field = knot_field + step_length * direction
        tie_residual = tie_residual - step_length * change
        gradient = adjoint(tie_residual) - damping * knot_field
        new_norm = slope_total(gradient)
        direction = gradient + new_norm / slope_norm * direction
        slope_norm = new_norm
    return (knot_field, tie_residual)


def solution(mesh):
    in_specs = (P("track", None, "det"), P("track", "det"), P("track"), P("track"), P("track"))
    out_specs = (P(None, "track"), P("track", "det"))
    return jax.shard_map(local, mesh=mesh, in_specs=in_specs, out_specs=out_specs, check_vma=False)
```

profile of v0, /device:TPU:1, one launch (start us, length us, event | category | flops | bytes accessed | tf_op | source)
XLA Modules:
  0.0 1151.5 jit_solution(3248454608757837504)
XLA Ops:
  1.5 3.8 sort.34
  5.3 3.5 gather_fusion.1
  9.5 13.1 %all-to-all-start.1 = ((s32[64,1,8]{2,1,0:T(1,128)}), s32[64,1,8]{2,1,0:T(1,128)S(1)}, u32[]{:S(2)}, u32[]{:S(2)}) async-start(s32[64,1,8]{2,1,0:T(1,128)} %bitcast.2), calls=%async_computation.1 | async-start | bytes 65536 | tf_op jit(solution)/shard_map/all_to_all | solution.py:29
  23.4 1.6 gather_fusion
  25.7 6.2 all-to-all-done.1
  32.0 5.5 all-to-all-start
  38.8 3.8 sort.35
  42.6 6.8 all-to-all-done
  49.4 2.6 gather_fusion.2
  53.7 7.9 fusion.14
  61.6 16.9 %psum.112 = f32[12,512]{0,1:T(8,128)} all-reduce(f32[12,512]{0,1:T(8,128)S(1)} %bitcast.110), channel_id=1, replica_groups=mesh['track'=64,'det'=4] {'det'}, use_global_device_ids=true, to_apply=%region_2.3 | all-reduce | flops 6144 | bytes 49152 | tf_op jit(solution)/shard_map/psum | solution.py:52
  78.5 1.2 convolution_bitcast_fusion.3
  79.7 7.5 collective-permute-start
  87.2 1.5 fusion.23
  89.7 1.9 collective-permute-start.1
  91.7 3.0 collective-permute-done.1
  95.8 6.3 fusion.12
  102.1 1.6 gather_fusion.3
  103.7 9.0 all-to-all-start.2
  113.4 124.9 %psum.113 = f32[]{:T(128)} all-reduce(f32[]{:T(128)} %multiply_reduce_fusion.10), channel_id=1, replica_groups=mesh['track'=64,'det'=4] {'track'}, use_global_device_ids=true, to_apply=%region_5.6 | all-reduce | flops 1 | bytes 8 | tf_op jit(solution)/shard_map/psum | solution.py:59
  238.4 2.6 gather_fusion.4
  241.0 2.3 multiply_reduce_fusion.3
  243.2 75.6 %all-reduce.3 = (f32[]{:T(128)}, f32[]{:T(128)}) all-reduce(f32[]{:T(128)} %get-tuple-element.77, f32[]{:T(128)} %multiply_reduce_fusion.10), channel_id=1, replica_groups=mesh['track'=64,'det'=4] {'track','det'}, use_global_device_ids=true, to_apply=%region_7.8 | all-reduce | flops 2 | bytes 16 | tf_op jit(solution)/shard_map/psum | solution.py:75
  320.7 1.1 multiply_subtract_fusion.3
  322.5 7.9 fusion.10
  330.4 16.5 %psum.116 = f32[12,512]{0,1:T(8,128)} all-reduce(f32[12,512]{0,1:T(8,128)S(1)} %bitcast.111), channel_id=1, replica_groups=mesh['track'=64,'det'=4] {'det'}, use_global_device_ids=true, to_apply=%region_9.10 | all-reduce | flops 6144 | bytes 49152 | tf_op jit(solution)/shard_map/psum | solution.py:52
  346.9 1.2 convolution_bitcast_fusion.2
  348.1 1.5 fusion.21
  349.6 8.1 collective-permute-start.2
  359.8 121.8 %psum.117 = f32[]{:T(128)} all-reduce(f32[]{:T(128)} %multiply_reduce_fusion.9), channel_id=1, replica_groups=mesh['track'=64,'det'=4] {'track'}, use_global_device_ids=true, to_apply=%region_11.12 | all-reduce | flops 1 | bytes 8 | tf_op jit(solution)/shard_map/psum | solution.py:59
  483.7 5.4 collective-permute-start.3
  490.8 6.3 fusion.8
  497.2 1.6 gather_fusion.5
  498.8 17.1 %all_to_all.34 = f32[64,8,128]{2,1,0:T(8,128)} all-to-all(f32[64,8,128]{2,1,0:T(8,128)} %bitcast.117), channel_id=1, replica_groups=mesh['track'=64,'det'=4] {'track'}, dimensions={0} | all-to-all | bytes 524288 | tf_op jit(solution)/shard_map/all_to_all | solution.py:40
  516.0 2.6 gather_fusion.6
  518.5 2.4 multiply_reduce_fusion.2
  520.9 75.0 %all-reduce.2 = (f32[]{:T(128)}, f32[]{:T(128)}) all-reduce(f32[]{:T(128)} %get-tuple-element.75, f32[]{:T(128)} %get-tuple-element.73), channel_id=1, replica_groups=mesh['track'=64,'det'=4] {'track','det'}, use_global_device_ids=true, to_apply=%region_13.14 | all-reduce | flops 2 | bytes 16 | tf_op jit(solution)/shard_map/psum | solution.py:75
  599.5 7.9 fusion.6
  607.4 15.1 %psum.120 = f32[12,512]{0,1:T(8,128)} all-reduce(f32[12,512]{0,1:T(8,128)S(1)} %bitcast.112), channel_id=1, replica_groups=mesh['track'=64,'det'=4] {'det'}, use_global_device_ids=true, to_apply=%region_16.17 | all-reduce | flops 6144 | bytes 49152 | tf_op jit(solution)/shard_map/psum | solution.py:52
  622.4 1.2 convolution_bitcast_fusion.1
  623.6 1.5 fusion.19
  625.1 8.4 collective-permute-start.4
  635.7 121.8 %psum.121 = f32[]{:T(128)} all-reduce(f32[]{:T(128)} %get-tuple-element.70), channel_id=1, replica_groups=mesh['track'=64,'det'=4] {'track'}, use_global_device_ids=true, to_apply=%region_18.19 | all-reduce | flops 1 | bytes 8 | tf_op jit(solution)/shard_map/psum | solution.py:59
  759.5 5.7 collective-permute-start.5
  766.7 6.3 fusion.4
  773.0 1.6 gather_fusion.7
  774.7 17.2 %all_to_all.35 = f32[64,8,128]{2,1,0:T(8,128)} all-to-all(f32[64,8,128]{2,1,0:T(8,128)} %bitcast.118), channel_id=1, replica_groups=mesh['track'=64,'det'=4] {'track'}, dimensions={0} | all-to-all | bytes 524288 | tf_op jit(solution)/shard_map/all_to_all | solution.py:40
  791.8 2.6 gather_fusion.8
  794.4 2.3 multiply_reduce_fusion.1
  796.8 74.7 %all-reduce.1 = (f32[]{:T(128)}, f32[]{:T(128)}) all-reduce(f32[]{:T(128)} %get-tuple-element.68, f32[]{:T(128)} %get-tuple-element.66), channel_id=1, replica_groups=mesh['track'=64,'det'=4] {'track','det'}, use_global_device_ids=true, to_apply=%region_20.21 | all-reduce | flops 2 | bytes 16 | tf_op jit(solution)/shard_map/psum | solution.py:75
  875.1 7.9 fusion.2
  883.0 15.2 %psum.124 = f32[12,512]{0,1:T(8,128)} all-reduce(f32[12,512]{0,1:T(8,128)S(1)} %bitcast.113), channel_id=1, replica_groups=mesh['track'=64,'det'=4] {'det'}, use_global_device_ids=true, to_apply=%region_23.24 | all-reduce | flops 6144 | bytes 49152 | tf_op jit(solution)/shard_map/psum | solution.py:52
  898.2 1.2 convolution_bitcast_fusion
  899.4 1.5 fusion.17
  900.9 8.5 collective-permute-start.6
  911.6 121.8 %psum.125 = f32[]{:T(128)} all-reduce(f32[]{:T(128)} %multiply_reduce_fusion.5), channel_id=1, replica_groups=mesh['track'=64,'det'=4] {'track'}, use_global_device_ids=true, to_apply=%region_25.26 | all-reduce | flops 1 | bytes 8 | tf_op jit(solution)/shard_map/psum | solution.py:59
  1035.6 5.4 collective-permute-start.7
  1042.7 6.3 fusion
  1049.1 1.6 gather_fusion.9
  1050.7 17.2 %all_to_all.36 = f32[64,8,128]{2,1,0:T(8,128)} all-to-all(f32[64,8,128]{2,1,0:T(8,128)} %bitcast.116), channel_id=1, replica_groups=mesh['track'=64,'det'=4] {'track'}, dimensions={0} | all-to-all | bytes 524288 | tf_op jit(solution)/shard_map/all_to_all | solution.py:40
  1067.9 2.6 gather_fusion.10
  1070.5 2.3 multiply_reduce_fusion
  1072.8 74.3 %all-reduce = (f32[]{:T(128)}, f32[]{:T(128)}) all-reduce(f32[]{:T(128)} %get-tuple-element.64, f32[]{:T(128)} %get-tuple-element.62), channel_id=1, replica_groups=mesh['track'=64,'det'=4] {'track','det'}, use_global_device_ids=true, to_apply=%region_27.28 | all-reduce | flops 2 | bytes 16 | tf_op jit(solution)/shard_map/psum | solution.py:75
  1149.6 1.8 multiply_subtract_fusion
  (72 shorter events, 27.3 us)
Async XLA Ops:
  0.6 53.1 %copy-start = (f32[512,12,128]{2,0,1:T(8,128)S(1)}, f32[512,12,128]{2,0,1:T(8,128)}, u32[]{:S(2)}) copy-start(f32[512,12,128]{2,0,1:T(8,128)} %param.13) | copy-start | bytes 9437188
  0.6 36.8 %copy-start.6 = (s32[512]{0:T(512)S(1)}, s32[512]{0:T(512)}, u32[]{:S(2)}) copy-start(s32[512]{0:T(512)} %param.16) | copy-start | bytes 6148
  0.7 22.7 %copy-start.1 = (f32[512,128]{1,0:T(8,128)S(1)}, f32[512,128]{1,0:T(8,128)}, u32[]{:S(2)}) copy-start(f32[512,128]{1,0:T(8,128)} %param.14) | copy-start | bytes 786436
  9.5 22.5 %all-to-all-start.1 = ((s32[64,1,8]{2,1,0:T(1,128)}), s32[64,1,8]{2,1,0:T(1,128)S(1)}, u32[]{:S(2)}, u32[]{:S(2)}) async-start(s32[64,1,8]{2,1,0:T(1,128)} %bitcast.2), calls=%async_computation.1 | async-start | bytes 65536 | tf_op jit(solution)/shard_map/all_to_all | solution.py:29
  32.0 17.4 %all-to-all-start = ((f32[64,8,128]{2,1,0:T(8,128)}), f32[64,8,128]{2,1,0:T(8,128)}, u32[]{:S(2)}, u32[]{:S(2)}) async-start(f32[64,8,128]{2,1,0:T(8,128)} %bitcast.114), calls=%async_computation | async-start | bytes 524288 | tf_op jit(solution)/shard_map/all_to_all | solution.py:40
  52.0 35.2 %copy-start.7 = (f32[512]{0:T(512)S(1)}, f32[512]{0:T(512)}, u32[]{:S(2)}) copy-start(f32[512]{0:T(512)} %param.17) | copy-start | bytes 6148
  53.0 0.7 copy-start.2
  79.7 9.0 collective-permute-start
  89.7 4.9 collective-permute-start.1
  103.7 134.6 %all-to-all-start.2 = ((f32[64,8,128]{2,1,0:T(8,128)}), f32[64,8,128]{2,1,0:T(8,128)}, u32[]{:S(2)}, u32[]{:S(2)}) async-start(f32[64,8,128]{2,1,0:T(8,128)} %bitcast.115), calls=%async_computation.2 | async-start | bytes 524288 | tf_op jit(solution)/shard_map/all_to_all | solution.py:40
  321.8 0.7 copy-start.5
  349.6 8.8 collective-permute-start.2
  483.7 6.0 collective-permute-start.3
  598.8 0.7 copy-start.4
  625.1 9.1 collective-permute-start.4
  759.5 6.0 collective-permute-start.5
  874.4 0.7 copy-start.3
  900.9 9.2 collective-permute-start.6
  1035.6 6.0 collective-permute-start.7
where the time goes:
time: 1160 us; the launch traced here: 1150 us
  blocking collectives  905 us (78%)
  starting transfers between devices  78.6 us (7%)
  matrix products  68.8 us (6%)
  other arithmetic  33.7 us (3%)
  local copies, waits for them, and re-layouts  33.2 us (3%)
  waiting for transfers between devices  19.6 us (2%)
  between operations  12.4 us (1%)
    psum x4, blocking collectives, slope_total(): return lax.psum(jnp.sum(gradient * gradient), 'track')  490 us
    psum x4, blocking collectives, local(): lax.psum((jnp.sum(change * change), jnp.sum(direction * direction)), ('tr...  300 us
    psum x4, blocking collectives, adjoint(): partial_value = lax.psum(partial_value, 'det')  63.7 us
    all_to_all x3, blocking collectives, partner_values(): lax.all_to_all(arrange(values), 'track', split_axis=0, concat_axis=0, til...  51.5 us
    ppermute x8, starting transfers between devices, passed_along(): lax.ppermute(value, axis, [(source, source + steps) for source in range(l...  51 us
    dot_general x4, matrix products, adjoint(): jnp.einsum('ipw,iw->pi', jac, residual_rows, precision=highest)  31.6 us
    dot_general x4, matrix products, local(): own_pred = jnp.einsum('ipw,pi->iw', jac, interp, precision=highest)  25.3 us
  transfers between devices with their start and end apart: 11, of which 9 were waited for; matrix products, arithmetic and copies ran while one was open for 1% of the time, Pallas kernels for 0%

commit v1 on v0

--- a/solution.py
+++ b/solution.py
@@ -49,7 +49,7 @@
 
     def adjoint(residual_rows):
         partial_value = jnp.einsum("ipw,iw->pi", jac, residual_rows, precision=highest)
-        partial_value = lax.psum(partial_value, "det")
+        partial_value = jnp.sum(lax.all_gather(partial_value, "det"), axis=0)
         spread = jnp.dot(partial_value, weights_back, precision=highest)
         spill_over = jnp.dot(partial_value, edge_weight, precision=highest)
         carried = passed_along(spill_over, "track", 1)

time: 1160 us -> 1130 us (0.974)
  blocking collectives: 905 us -> 882 us
    psum x4 -> x0, blocking collectives: 63.7 us -> none  [adjoint(): partial_value = lax.psum(partial_value, 'det')]
    all_gather x0 -> x4, blocking collectives: none -> 37.4 us  [adjoint(): partial_value = jnp.sum(lax.all_gather(partial_value, 'det'), axis=0)]
  transfers between devices with their start and end apart: 11 -> 11, of which waited for: 9 -> 10; matrix products, arithmetic and copies ran while one was open for 1% -> 1% of each run, Pallas kernels for 0% -> 0%
where the time goes in v1:
time: 1130 us; the launch traced here: 1120 us
  blocking collectives  882 us (78%)
  starting transfers between devices  74.3 us (7%)
  matrix products  59.7 us (5%)
  other arithmetic  33.8 us (3%)
  local copies, waits for them, and re-layouts  33.7 us (3%)
  waiting for transfers between devices  20.5 us (2%)
  between operations  12.3 us (1%)
    psum x4, blocking collectives, slope_total(): return lax.psum(jnp.sum(gradient * gradient), 'track')  493 us
    psum x4, blocking collectives, local(): lax.psum((jnp.sum(change * change), jnp.sum(direction * direction)), ('tr...  300 us
    all_to_all x3, blocking collectives, partner_values(): lax.all_to_all(arrange(values), 'track', split_axis=0, concat_axis=0, til...  51.4 us
    ppermute x8, starting transfers between devices, passed_along(): lax.ppermute(value, axis, [(source, source + steps) for source in range(l...  46.6 us
    all_gather x4, blocking collectives, adjoint(): partial_value = jnp.sum(lax.all_gather(partial_value, 'det'), axis=0)  37.4 us
    dot_general x4, matrix products, adjoint(): jnp.einsum('ipw,iw->pi', jac, residual_rows, precision=highest)  31.6 us
    dot_general x4, matrix products, local(): own_pred = jnp.einsum('ipw,pi->iw', jac, interp, precision=highest)  25.3 us
  transfers between devices with their start and end apart: 11, of which 10 were waited for; matrix products, arithmetic and copies ran while one was open for 1% of the time, Pallas kernels for 0%

profile of v1, /device:TPU:1, one launch (start us, length us, event | category | flops | bytes accessed | tf_op | source)
XLA Modules:
  0.0 1116.4 jit_solution(16090305261838818245)
XLA Ops:
  0.7 0.9 add_select_fusion.4
  1.5 3.8 sort.34
  5.3 3.5 gather_fusion.1
  9.5 13.1 %all-to-all-start.1 = ((s32[64,1,8]{2,1,0:T(1,128)}), s32[64,1,8]{2,1,0:T(1,128)S(1)}, u32[]{:S(2)}, u32[]{:S(2)}) async-start(s32[64,1,8]{2,1,0:T(1,128)} %bitcast.2), calls=%async_computation.1 | async-start | bytes 65536 | tf_op jit(solution)/shard_map/all_to_all | solution.py:29
  23.4 1.6 gather_fusion
  25.7 6.2 all-to-all-done.1
  32.0 5.5 all-to-all-start
  38.8 3.8 sort.35
  42.6 6.8 all-to-all-done
  49.4 2.6 gather_fusion.2
  52.0 1.0 sub.50
  53.7 7.9 fusion.14
  61.7 9.9 all-gather.4
  71.8 6.3 collective-permute-start
  79.7 1.9 collective-permute-start.1
  81.7 3.5 collective-permute-done.1
  85.4 0.9 copy.23
  86.3 6.3 fusion.12
  92.6 1.6 gather_fusion.3
  94.3 9.1 all-to-all-start.2
  104.0 124.9 %psum.84 = f32[]{:T(128)} all-reduce(f32[]{:T(128)} %multiply_reduce_fusion.10), channel_id=1, replica_groups=mesh['track'=64,'det'=4] {'track'}, use_global_device_ids=true, to_apply=%region_5.6 | all-reduce | flops 1 | bytes 8 | tf_op jit(solution)/shard_map/psum | solution.py:59
  228.9 2.6 gather_fusion.4
  231.5 2.3 multiply_reduce_fusion.3
  233.8 77.9 %all-reduce.3 = (f32[]{:T(128)}, f32[]{:T(128)}) all-reduce(f32[]{:T(128)} %get-tuple-element.77, f32[]{:T(128)} %multiply_reduce_fusion.10), channel_id=1, replica_groups=mesh['track'=64,'det'=4] {'track','det'}, use_global_device_ids=true, to_apply=%region_7.8 | all-reduce | flops 2 | bytes 16 | tf_op jit(solution)/shard_map/psum | solution.py:75
  313.6 1.1 multiply_subtract_fusion.3
  315.4 7.9 fusion.10
  323.4 9.1 all-gather.5
  332.9 7.6 collective-permute-start.2
  342.7 121.8 %psum.87 = f32[]{:T(128)} all-reduce(f32[]{:T(128)} %multiply_reduce_fusion.9), channel_id=1, replica_groups=mesh['track'=64,'det'=4] {'track'}, use_global_device_ids=true, to_apply=%region_11.12 | all-reduce | flops 1 | bytes 8 | tf_op jit(solution)/shard_map/psum | solution.py:59
  466.5 5.4 collective-permute-start.3
  472.9 0.9 copy.27
  473.7 6.3 fusion.8
  480.0 1.6 gather_fusion.5
  481.7 17.1 %all_to_all.34 = f32[64,8,128]{2,1,0:T(8,128)} all-to-all(f32[64,8,128]{2,1,0:T(8,128)} %bitcast.117), channel_id=1, replica_groups=mesh['track'=64,'det'=4] {'track'}, dimensions={0} | all-to-all | bytes 524288 | tf_op jit(solution)/shard_map/all_to_all | solution.py:40
  498.8 2.6 gather_fusion.6
  501.4 2.4 multiply_reduce_fusion.2
  503.8 74.6 %all-reduce.2 = (f32[]{:T(128)}, f32[]{:T(128)}) all-reduce(f32[]{:T(128)} %get-tuple-element.75, f32[]{:T(128)} %get-tuple-element.73), channel_id=1, replica_groups=mesh['track'=64,'det'=4] {'track','det'}, use_global_device_ids=true, to_apply=%region_13.14 | all-reduce | flops 2 | bytes 16 | tf_op jit(solution)/shard_map/psum | solution.py:75
  580.3 1.1 multiply_subtract_fusion.2
  582.0 7.9 fusion.6
  590.0 9.2 all-gather.6
  599.7 7.1 collective-permute-start.4
  609.0 122.8 %psum.90 = f32[]{:T(128)} all-reduce(f32[]{:T(128)} %get-tuple-element.70), channel_id=1, replica_groups=mesh['track'=64,'det'=4] {'track'}, use_global_device_ids=true, to_apply=%region_18.19 | all-reduce | flops 1 | bytes 8 | tf_op jit(solution)/shard_map/psum | solution.py:59
  733.8 5.7 collective-permute-start.5
  740.2 0.9 copy.31
  741.0 6.3 fusion.4
  747.4 1.6 gather_fusion.7
  749.0 17.1 %all_to_all.35 = f32[64,8,128]{2,1,0:T(8,128)} all-to-all(f32[64,8,128]{2,1,0:T(8,128)} %bitcast.118), channel_id=1, replica_groups=mesh['track'=64,'det'=4] {'track'}, dimensions={0} | all-to-all | bytes 524288 | tf_op jit(solution)/shard_map/all_to_all | solution.py:40
  766.2 2.6 gather_fusion.8
  768.7 2.4 multiply_reduce_fusion.1
  771.1 73.8 %all-reduce.1 = (f32[]{:T(128)}, f32[]{:T(128)}) all-reduce(f32[]{:T(128)} %get-tuple-element.68, f32[]{:T(128)} %get-tuple-element.66), channel_id=1, replica_groups=mesh['track'=64,'det'=4] {'track','det'}, use_global_device_ids=true, to_apply=%region_20.21 | all-reduce | flops 2 | bytes 16 | tf_op jit(solution)/shard_map/psum | solution.py:75
  846.7 1.1 multiply_subtract_fusion.1
  848.4 7.9 fusion.2
  856.4 9.2 all-gather.7
  866.1 7.1 collective-permute-start.6
  875.4 123.7 %psum.93 = f32[]{:T(128)} all-reduce(f32[]{:T(128)} %multiply_reduce_fusion.5), channel_id=1, replica_groups=mesh['track'=64,'det'=4] {'track'}, use_global_device_ids=true, to_apply=%region_25.26 | all-reduce | flops 1 | bytes 8 | tf_op jit(solution)/shard_map/psum | solution.py:59
  1001.1 5.5 collective-permute-start.7
  1007.5 0.9 copy.35
  1008.3 6.3 fusion
  1014.7 1.6 gather_fusion.9
  1016.3 17.2 %all_to_all.36 = f32[64,8,128]{2,1,0:T(8,128)} all-to-all(f32[64,8,128]{2,1,0:T(8,128)} %bitcast.116), channel_id=1, replica_groups=mesh['track'=64,'det'=4] {'track'}, dimensions={0} | all-to-all | bytes 524288 | tf_op jit(solution)/shard_map/all_to_all | solution.py:40
  1033.5 2.6 gather_fusion.10
  1036.1 2.3 multiply_reduce_fusion
  1038.4 73.6 %all-reduce = (f32[]{:T(128)}, f32[]{:T(128)}) all-reduce(f32[]{:T(128)} %get-tuple-element.64, f32[]{:T(128)} %get-tuple-element.62), channel_id=1, replica_groups=mesh['track'=64,'det'=4] {'track','det'}, use_global_device_ids=true, to_apply=%region_27.28 | all-reduce | flops 2 | bytes 16 | tf_op jit(solution)/shard_map/psum | solution.py:75
  1114.5 1.8 multiply_subtract_fusion
  (80 shorter events, 22.7 us)
Async XLA Ops:
  0.6 53.1 %copy-start = (f32[512,12,128]{2,0,1:T(8,128)S(1)}, f32[512,12,128]{2,0,1:T(8,128)}, u32[]{:S(2)}) copy-start(f32[512,12,128]{2,0,1:T(8,128)} %param.13) | copy-start | bytes 9437188
  0.6 36.8 %copy-start.6 = (s32[512]{0:T(512)S(1)}, s32[512]{0:T(512)}, u32[]{:S(2)}) copy-start(s32[512]{0:T(512)} %param.16) | copy-start | bytes 6148
  0.7 22.7 %copy-start.1 = (f32[512,128]{1,0:T(8,128)S(1)}, f32[512,128]{1,0:T(8,128)}, u32[]{:S(2)}) copy-start(f32[512,128]{1,0:T(8,128)} %param.14) | copy-start | bytes 786436
  9.5 22.5 %all-to-all-start.1 = ((s32[64,1,8]{2,1,0:T(1,128)}), s32[64,1,8]{2,1,0:T(1,128)S(1)}, u32[]{:S(2)}, u32[]{:S(2)}) async-start(s32[64,1,8]{2,1,0:T(1,128)} %bitcast.2), calls=%async_computation.1 | async-start | bytes 65536 | tf_op jit(solution)/shard_map/all_to_all | solution.py:29
  32.0 17.4 %all-to-all-start = ((f32[64,8,128]{2,1,0:T(8,128)}), f32[64,8,128]{2,1,0:T(8,128)}, u32[]{:S(2)}, u32[]{:S(2)}) async-start(f32[64,8,128]{2,1,0:T(8,128)} %bitcast.114), calls=%async_computation | async-start | bytes 524288 | tf_op jit(solution)/shard_map/all_to_all | solution.py:40
  52.0 26.1 %copy-start.7 = (f32[512]{0:T(512)S(1)}, f32[512]{0:T(512)}, u32[]{:S(2)}) copy-start(f32[512]{0:T(512)} %param.17) | copy-start | bytes 6148
  53.0 0.7 copy-start.2
  71.8 7.0 collective-permute-start
  79.7 5.4 collective-permute-start.1
  94.3 134.7 %all-to-all-start.2 = ((f32[64,8,128]{2,1,0:T(8,128)}), f32[64,8,128]{2,1,0:T(8,128)}, u32[]{:S(2)}, u32[]{:S(2)}) async-start(f32[64,8,128]{2,1,0:T(8,128)} %bitcast.115), calls=%async_computation.2 | async-start | bytes 524288 | tf_op jit(solution)/shard_map/all_to_all | solution.py:40
  314.6 0.7 copy-start.5
  332.9 8.3 collective-permute-start.2
  466.5 6.0 collective-permute-start.3
  581.3 0.7 copy-start.4
  599.7 7.8 collective-permute-start.4
  733.8 6.1 collective-permute-start.5
  847.7 0.7 copy-start.3
  866.1 7.8 collective-permute-start.6
  1001.1 6.1 collective-permute-start.7
